TPU v7x, 512 devices: a whole 4x8x8 slice. The times are simulated.
512 devices in a mesh: fsdp: 64 (over z, x, y_lo), tp: 8 (over y_hi, core).
Axes of the slice: x: 4, y: 8 (y_hi: 4, y_lo: 2; y = y_hi * 2 + y_lo), z: 8, core: 2. Of those that a mesh axis runs over, the one named last changes fastest.
Arguments:
- gate_pre: bfloat16 [8192, 14336], P('fsdp', 'tp'), may hold values from -6 to 6
- up_pre: bfloat16 [8192, 14336], P('fsdp', 'tp'), may hold values from -6 to 6
- down_weight: bfloat16 [14336, 4096], P('tp', 'fsdp'), may hold values from -0.046875 to 0.046875
Outputs:
- mixed: bfloat16 [8192, 4096], P('fsdp', 'tp')
All inputs are finite; a program needn't handle non-finite values.
Results may differ from a plain program's by a relative error of at most 0.0049.
Values may be sent and summed in bfloat16 or wider, within the bound.
A program may use at most 64 MiB of HBM per device.

v0:
```python
import jax
import jax.numpy as jnp
from jax import lax
from jax.sharding import PartitionSpec as P


def shards(gate_pre, up_pre, down_weight):
    hidden = (jax.nn.silu(gate_pre.astype(jnp.float32)) * up_pre.astype(jnp.float32)).astype(
        jnp.bfloat16
    )
    terms = jnp.dot(
        hidden,
        lax.all_gather(down_weight, "fsdp", axis=1, tiled=True),
        preferred_element_type=jnp.float32,
    )
    totals = lax.psum(terms, "tp")
    share = totals.shape[1] // lax.axis_size("tp")
    result = lax.dynamic_slice_in_dim(totals, lax.axis_index("tp") * share, share, 1)
    return result.astype(jnp.bfloat16)


def solution(mesh):
    return jax.shard_map(
        shards,
        mesh=mesh,
        in_specs=(P("fsdp", "tp"), P("fsdp", "tp"), P("tp", "fsdp")),
        out_specs=P("fsdp", "tp"),
        check_vma=False,
    )
```

profile of v0, /device:TPU:1, one launch (start us, length us, event | category | flops | bytes accessed | tf_op | source)
XLA Modules:
  0.0 456.0 jit_solution(7326851797001008196)
XLA Ops:
  6.5 0.0 all-gather.2.cloned.1.call-start
  6.5 0.7 all-gather.2.cloned.1.call-update
  7.3 331.1 %all-gather.2.cloned.1.call-done = bf16[1792,4096]{0,1:T(8,128)(2,1)} async-done(((bf16[1792,64]{0,1:T(8,128)(2,1)}), bf16[1792,4096]{0,1:T(8,128)(2,1)}) %all-gather.2.cloned.1.call-update) | async-done | bytes 14680080 | tf_op jit(solution)/shard_map/all_gather | solution.py:13
  338.4 10.2 %fusion.5 = f32[128,4096]{1,0:T(8,128)S(1)} fusion(bf16[1792,4096]{0,1:T(8,128)(2,1)} %all-gather.2.cloned.1.call-done, bf16[128,1792]{1,0:T(8,128)(2,1)} %param.4, bf16[128,1792]{1,0:T(8,128)(2,1)} %param.3), kind=kOutput, calls=%fused_computation.7 | convolution fusion | flops 1880883200 | bytes 17694720 | tf_op jit(solution)/shard_map/dot_general | solution.py:11
  348.7 99.8 %all-reduce.1 = bf16[128,4096]{1,0:T(8,128)(2,1)S(1)} all-reduce(f32[128,4096]{1,0:T(8,128)S(1)} %fusion.5), channel_id=1, replica_groups=mesh['fsdp'=64,'tp'=8] {'tp'}, use_global_device_ids=true, to_apply=%region_0.1 | all-reduce | flops 524288 | bytes 3145728 | tf_op jit(solution)/shard_map/psum | solution.py:16
  448.5 0.7 dynamic-slice_convert_fusion
Async XLA Ops:
  6.5 331.9 %all-gather.2.cloned.1.call-start = ((), (), s32[]{:S(2)}) async-start(), calls=%async_computation | async-start | bytes 14909440 | tf_op jit(solution)/shard_map/all_gather | solution.py:13
Sparse Core Ops, SparseCore 0:
  9.4 328.9 all-gather.1
where the time goes:
time: 456 us
  waiting for transfers between devices  332 us (73%)
  blocking collectives  99.8 us (22%)
  between operations  13.4 us (3%)
  matrix products  10.2 us (2%)
    all_gather x1, waiting for transfers between devices, shards(): lax.all_gather(down_weight, 'fsdp', axis=1, tiled=True)  331 us
    psum x1, blocking collectives, shards(): totals = lax.psum(terms, 'tp')  99.8 us
    dot_general x1, matrix products, shards(): jnp.dot(hidden, lax.all_gather(down_weight, 'fsdp', axis=1, tiled=True),...  10.2 us
  transfers between devices with their start and end apart: 1, of which 1 were waited for; matrix products, arithmetic and copies ran while one was open for 0% of the time, Pallas kernels for 0%

commit v1 on v0

--- a/solution.py
+++ b/solution.py
@@ -13,7 +13,7 @@
         lax.all_gather(down_weight, "fsdp", axis=1, tiled=True),
         preferred_element_type=jnp.float32,
     )
-    totals = lax.psum(terms, "tp")
+    totals = jnp.sum(lax.all_gather(terms, "tp"), axis=0)
     share = totals.shape[1] // lax.axis_size("tp")
     result = lax.dynamic_slice_in_dim(totals, lax.axis_index("tp") * share, share, 1)
     return result.astype(jnp.bfloat16)

time: 456 us -> 557 us (1.22)
  waiting for transfers between devices: 332 us -> 524 us
  blocking collectives: 99.8 us -> 0 us
  other arithmetic: 0 us -> 7.49 us
    all_gather x0 -> x1, waiting for transfers between devices: none -> 192 us  [shards(): totals = jnp.sum(lax.all_gather(terms, 'tp'), axis=0)]
    psum x1 -> x0, blocking collectives: 99.8 us -> none  [shards(): totals = lax.psum(terms, 'tp')]
    reduce_sum x0 -> x1, other arithmetic: none -> 7.49 us  [shards(): totals = jnp.sum(lax.all_gather(terms, 'tp'), axis=0)]
  transfers between devices with their start and end apart: 1 -> 2, of which waited for: 1 -> 2; matrix products, arithmetic and copies ran while one was open for 0% -> 0% of each run, Pallas kernels for 0% -> 0%
where the time goes in v1:
time: 557 us
  waiting for transfers between devices  524 us (94%)
  between operations  13.4 us (2%)
  matrix products  11.6 us (2%)
  other arithmetic  7.49 us (1%)
    all_gather x1, waiting for transfers between devices, shards(): lax.all_gather(down_weight, 'fsdp', axis=1, tiled=True)  331 us
    all_gather x1, waiting for transfers between devices, shards(): totals = jnp.sum(lax.all_gather(terms, 'tp'), axis=0)  192 us
    dot_general x1, matrix products, shards(): jnp.dot(hidden, lax.all_gather(down_weight, 'fsdp', axis=1, tiled=True),...  11.6 us
  transfers between devices with their start and end apart: 2, of which 2 were waited for; matrix products, arithmetic and copies ran while one was open for 0% of the time, Pallas kernels for 0%

profile of v1, /device:TPU:1, one launch (start us, length us, event | category | flops | bytes accessed | tf_op | source)
XLA Modules:
  0.0 557.0 jit_solution(9738195290681244394)
XLA Ops:
  6.5 0.0 all-gather.4.cloned.1.call-start
  6.5 0.7 all-gather.4.cloned.1.call-update
  7.3 0.0 all-gather.6.cloned.1.call-start
  7.3 331.1 %all-gather.4.cloned.1.call-done = bf16[1792,4096]{0,1:T(8,128)(2,1)} async-done(((bf16[1792,64]{0,1:T(8,128)(2,1)}), bf16[1792,4096]{0,1:T(8,128)(2,1)}) %all-gather.4.cloned.1.call-update) | async-done | bytes 14680080 | tf_op jit(solution)/shard_map/all_gather | solution.py:13
  338.4 11.6 %fusion.5 = f32[128,4096]{1,0:T(8,128)} fusion(bf16[1792,4096]{0,1:T(8,128)(2,1)} %all-gather.4.cloned.1.call-done, bf16[128,1792]{1,0:T(8,128)(2,1)} %param.4, bf16[128,1792]{1,0:T(8,128)(2,1)} %param.3), kind=kOutput, calls=%fused_computation.7 | convolution fusion | flops 1880883200 | bytes 17694720 | tf_op jit(solution)/shard_map/dot_general | solution.py:11
  350.0 0.0 all-gather.6.cloned.1.call-update
  350.0 192.0 %all-gather.6.cloned.1.call-done = f32[1024,4096]{1,0:T(8,128)} async-done(((f32[128,4096]{1,0:T(8,128)}), f32[1024,4096]{1,0:T(8,128)}) %all-gather.6.cloned.1.call-update) | async-done | bytes 16777232 | tf_op jit(solution)/shard_map/all_gather | solution.py:16
  542.0 7.5 %reduce_sum.9 = bf16[128,4096]{1,0:T(8,128)(2,1)S(1)} reduce(f32[8,128,4096]{2,1,0:T(8,128)} %bitcast.2, f32[]{:T(128)} %constant.2.clone.1), dimensions={0}, to_apply=%region_0.1 | reduce | flops 3670016 | bytes 17825796 | tf_op jit(solution)/shard_map/reduce_sum | solution.py:16
  549.5 0.7 dynamic-slice_convert_fusion
Async XLA Ops:
  6.5 331.9 %all-gather.4.cloned.1.call-start = ((), (), s32[]{:S(2)}) async-start(), calls=%async_computation | async-start | bytes 14909440 | tf_op jit(solution)/shard_map/all_gather | solution.py:13
  7.3 534.8 %all-gather.6.cloned.1.call-start = ((), (), s32[]{:S(2)}) async-start(), calls=%async_computation.1 | async-start | bytes 18874368 | tf_op jit(solution)/shard_map/all_gather | solution.py:16
Sparse Core Ops, SparseCore 0:
  9.4 328.9 all-gather.3
  350.2 191.8 all-gather.5
